TPU v7x, 32 devices: a whole 2x2x4 slice. The times are simulated.
32 devices in a mesh: sens: 4 (over y, core), par: 8 (over z, x).
Axes of the slice: x: 2, y: 2, z: 4, core: 2. Of those that a mesh axis runs over, the one named last changes fastest.
Arguments:
- probes: float32 [2048, 512], P('par', 'sens'), may hold values from -6 to 6
- kernel: float32 [64, 2048, 2048], P(None, 'par', 'sens'), may hold values from -0.015625 to 0.015625
- noise_inverse: float32 [64, 64], replicated, may hold values from -1 to 3, as said below
- sensor_weight: float32 [2048], P('sens'), may hold values from 0.25 to 4
Outputs:
- hessian_action: float32 [2048, 512], P('par', 'sens')
Inputs may be any that keep to these rules, and one draw needn't show every extreme that they name: `noise_inverse`: symmetric.
All inputs are finite; a program needn't handle non-finite values.
Results may differ from a plain program's by a relative error of at most 0.0001.
Values sent between devices are 32-bit elements; how exact they have to be, the bound alone decides.
A program may use at most 192 MiB of HBM per device.

v0:
```python
import jax
import jax.numpy as jnp
from jax import lax
from jax.sharding import PartitionSpec as P


def apply_noise(observed, noise_inverse, weights_part):
    time_steps = noise_inverse.shape[0]
    row_count = observed.shape[0]
    columns = observed.shape[1]
    probe_count = columns // time_steps
    mixed = jnp.einsum(
        "tu,rup->rtp",
        noise_inverse,
        observed.reshape(row_count, time_steps, probe_count),
        precision=lax.Precision.HIGHEST,
        preferred_element_type=jnp.float32,
    )
    return mixed.reshape(row_count, columns) * weights_part[:, None]


def per_device(probes, kernel, noise_inverse, sensor_weight):
    highest = lax.Precision.HIGHEST
    time_steps = noise_inverse.shape[0]
    par_rows = kernel.shape[1]
    sensor_rows = kernel.shape[2]
    gathered = lax.all_gather(probes, "sens", axis=1, tiled=True)
    columns = gathered.shape[1]
    probe_count = columns // time_steps
    lag_list = jnp.arange(time_steps, dtype=jnp.int32)
    probe_field = gathered.reshape(par_rows, time_steps, probe_count)
    padded = jnp.pad(probe_field, ((0, 0), (time_steps, 0), (0, 0)))
    shifted = jax.vmap(
        lambda lag_index: lax.dynamic_slice_in_dim(padded, time_steps - lag_index, time_steps, 1)
    )(lag_list)
    shifted = shifted.reshape(time_steps * par_rows, columns)
    kernel_flat = kernel.reshape(time_steps * par_rows, sensor_rows)
    observed = lax.psum(
        lax.dot_general(
            kernel_flat,
            shifted,
            (((0,), (0,)), ((), ())),
            precision=highest,
            preferred_element_type=jnp.float32,
        ),
        "par",
    )
    weighted = apply_noise(observed, noise_inverse, sensor_weight)
    spread = jnp.dot(kernel_flat, weighted, precision=highest, preferred_element_type=jnp.float32)
    spread = spread.reshape(time_steps, par_rows, time_steps, probe_count)
    spread = jnp.pad(spread, ((0, 0), (0, 0), (0, time_steps), (0, 0)))
    earlier = jax.vmap(
        lambda lag_index, spread_lag: lax.dynamic_slice_in_dim(spread_lag, lag_index, time_steps, 1)
    )(lag_list, spread)
    partial_action = jnp.sum(earlier, axis=0).reshape(par_rows, columns)
    return lax.psum_scatter(partial_action, "sens", scatter_dimension=1, tiled=True)


def solution(mesh):
    placed = (P("par", "sens"), P(None, "par", "sens"), P(), P("sens"))
    return jax.shard_map(
        per_device, mesh=mesh, in_specs=placed, out_specs=P("par", "sens"), check_vma=False
    )
```

profile of v0, /device:TPU:31, one launch (start us, length us, event | category | flops | bytes accessed | tf_op | source)
XLA Modules:
  0.0 382.9 jit_solution(18350455227493733736)
XLA Ops:
  6.5 0.0 copy-start
  6.5 0.0 all-reduce.4.cloned.1.call-start
  6.5 7.5 %all_gather.3 = f32[256,512]{1,0:T(8,128)S(1)} all-gather(f32[256,128]{1,0:T(8,128)} %param.4), channel_id=1, replica_groups=mesh['sens'=4,'par'=8] {'sens'}, dimensions={1}, use_global_device_ids=true | all-gather | bytes 655360 | tf_op jit(solution)/shard_map/all_gather | solution.py:27
  14.0 0.2 copy.7
  14.2 0.1 pad.8
  14.3 12.4 %gather_fusion = f32[64,256,64,8]{1,3,2,0:T(8,128)} fusion(f32[256,128,8]{0,2,1:T(8,128)S(1)} %pad.8, s32[64]{0:T(128)S(1)} %fusion.7), kind=kCustom, calls=%fused_computation | custom fusion | bytes 67109632 | tf_op jit(solution)/shard_map/vmap()/gather | solution.py:34
  26.7 28.2 %copy.18 = f32[64,256,64,8]{1,0,3,2:T(8,128)S(1)} copy(f32[64,256,64,8]{1,3,2,0:T(8,128)} %gather_fusion) | data formatting | bytes 67108864 | tf_op jit(solution)/shard_map/vmap()/gather | solution.py:34
  54.9 25.6 %copy.12 = f32[64,8,64,256]{3,1,2,0:T(8,128)} copy(f32[64,8,64,256]{3,2,1,0:T(8,128)S(1)} %bitcast.37) | data formatting | bytes 67108864
  80.5 0.0 copy-start.2
  80.5 58.3 %convolution_bitcast_fusion = f32[512,64,8]{0,2,1:T(8,128)S(1)} fusion(f32[16384,512]{0,1:T(8,128)} %bitcast.35, f32[16384,512]{1,0:T(8,128)} %bitcast.33), kind=kOutput, calls=%fused_computation.3 | convolution fusion | flops 51539607552 | bytes 68157440 | tf_op jit(solution)/shard_map/dot_general | solution.py:39
  138.9 1.6 copy.9
  140.5 0.0 all-reduce.4.cloned.1.call-update
  140.5 0.0 reduce-scatter.2.cloned.1.call-start
  140.6 76.8 %all-reduce.4.cloned.1.call-done = f32[512,64,8]{0,1,2:T(8,128)} async-done(((f32[512,64,8]{0,1,2:T(8,128)}), f32[512,64,8]{0,1,2:T(8,128)}) %all-reduce.4.cloned.1.call-update) | async-done | bytes 1048592 | tf_op jit(solution)/shard_map/psum | solution.py:38
  217.4 0.0 copy-done
  217.4 0.0 copy-done.2
  217.4 2.3 fusion
  219.7 63.4 %fusion.1 = f32[512,16384]{1,0:T(8,128)} fusion(f32[16384,512]{1,0:T(8,128)} %bitcast.34, f32[512,64,8]{0,1,2:T(8,128)S(1)} %fusion), kind=kOutput, calls=%fused_computation.6 | convolution fusion | flops 51539607552 | bytes 68157440 | tf_op jit(solution)/shard_map/dot_general | solution.py:49
  283.1 32.6 %pad.9 = f32[64,256,128,8]{1,3,0,2:T(8,128)} pad(f32[64,256,64,8]{1,3,0,2:T(8,128)} %bitcast.36, f32[]{:T(128)} %constant.4.clone.1), padding=0_0x0_0x0_64x0_0 | pad | bytes 100663296 | tf_op jit(solution)/shard_map/jit(_pad)/pad | solution.py:51
  315.7 0.0 copy-start.1
  315.7 23.7 %gather_fusion.1 = f32[64,256,64,8]{1,3,2,0:T(8,128)} fusion(f32[64,256,128,8]{1,3,0,2:T(8,128)} %pad.9, s32[64]{0:T(128)S(1)} %fusion.10), kind=kCustom, calls=%fused_computation.1 | custom fusion | bytes 67109888 | tf_op jit(solution)/shard_map/vmap()/gather | solution.py:53
  339.4 12.7 %reduce_sum.9 = f32[256,64,8]{0,2,1:T(8,128)} reduce(f32[64,256,64,8]{1,3,2,0:T(8,128)} %gather_fusion.1, f32[]{:T(128)} %constant.4.clone.1), dimensions={0}, to_apply=%region_1.2 | reduce | flops 8257536 | bytes 34078724 | tf_op jit(solution)/shard_map/reduce_sum | solution.py:55
  352.0 0.0 reduce-scatter.2.cloned.1.call-update
  352.1 22.3 %reduce-scatter.2.cloned.1.call-done = f32[256,128]{0,1:T(8,128)} async-done(((f32[256,512]{0,1:T(8,128)}), f32[256,128]{0,1:T(8,128)}) %reduce-scatter.2.cloned.1.call-update) | async-done | bytes 131088 | tf_op jit(solution)/shard_map/reduce_scatter | solution.py:56
  374.4 1.7 copy.11
  376.0 0.0 copy-done.1
  (2 shorter events, 0.0 us)
Async XLA Ops:
  6.5 210.8 %copy-start = (f32[64,64]{1,0:T(8,128)S(1)}, f32[64,64]{1,0:T(8,128)}, u32[]{:S(2)}) copy-start(f32[64,64]{1,0:T(8,128)} %param.6) | copy-start | bytes 49156
  6.5 210.8 %all-reduce.4.cloned.1.call-start = ((), (), s32[]{:S(2)}) async-start(), calls=%async_computation.1 | async-start | bytes 2097152 | tf_op jit(solution)/shard_map/psum | solution.py:38
  80.5 136.9 %copy-start.2 = (f32[512]{0:T(512)S(1)}, f32[512]{0:T(512)}, u32[]{:S(2)}) copy-start(f32[512]{0:T(512)} %param.7) | copy-start | bytes 6148
  140.5 233.8 %reduce-scatter.2.cloned.1.call-start = ((), (), s32[]{:S(2)}) async-start(), calls=%async_computation.2 | async-start | bytes 655360 | tf_op jit(solution)/shard_map/reduce_scatter | solution.py:56
  315.7 60.3 %copy-start.1 = (f32[64,64]{1,0:T(8,128)S(1)}, f32[64,64]{1,0:T(8,128)}, u32[]{:S(2)}) copy-start(f32[64,64]{1,0:T(8,128)} %param.6) | copy-start | bytes 49156
Sparse Core Ops, SparseCore 0:
  140.6 76.6 all-reduce.3
  352.2 22.1 reduce-scatter.1
where the time goes:
time: 386 us; the launch traced here: 383 us
  local copies, waits for them, and re-layouts  126 us (33%)
  matrix products  124 us (32%)
  waiting for transfers between devices  99.1 us (26%)
  between operations  13.5 us (3%)
  other arithmetic  12.7 us (3%)
  blocking collectives  7.49 us (2%)
    psum x1, waiting for transfers between devices, per_device(): lax.psum(lax.dot_general(kernel_flat, shifted, (((0,), (0,)), ((), ())),...  76.8 us
    dot_general x1, matrix products, per_device(): jnp.dot(kernel_flat, weighted, precision=highest, preferred_element_type=...  63.4 us
    dot_general x1, matrix products, per_device(): lax.dot_general(kernel_flat, shifted, (((0,), (0,)), ((), ())), precision...  58.3 us
    gather x2, local copies, waits for them, and re-layouts, per_device(): lax.dynamic_slice_in_dim(padded, time_steps - lag_index, time_steps, 1)  40.6 us
    pad x1, local copies, waits for them, and re-layouts, per_device(): spread = jnp.pad(spread, ((0, 0), (0, 0), (0, time_steps), (0, 0)))  32.6 us
    unnamed x7, local copies, waits for them, and re-layouts  25.6 us
    gather x1, local copies, waits for them, and re-layouts, per_device(): lax.dynamic_slice_in_dim(spread_lag, lag_index, time_steps, 1)  23.7 us
    reduce_scatter x1, waiting for transfers between devices, per_device(): lax.psum_scatter(partial_action, 'sens', scatter_dimension=1, tiled=True)  22.3 us
  transfers between devices with their start and end apart: 2, of which 2 were waited for; matrix products, arithmetic and copies ran while one was open for 0% of the time, Pallas kernels for 0%

commit v1 on v0

v1 whole, which is shorter than its diff:
```python
import functools

import jax
import jax.numpy as jnp
from jax import lax
from jax.experimental import pallas as pl
from jax.experimental.pallas import tpu as pltpu
from jax.sharding import PartitionSpec as P

MESH = pl.DeviceIdType.MESH
LAGS = 4
SLOTS = 8
F32 = jnp.float32
BF16 = jnp.bfloat16


def split(value):
    high = value.astype(BF16)
    return high, (value - high.astype(F32)).astype(BF16)


def dot3(left, right, transposed=False):
    dims = (((1,), (1 if transposed else 0,)), ((), ()))
    (lh, ll), (rh, rl) = left, right
    mul = functools.partial(lax.dot_general, dimension_numbers=dims, preferred_element_type=F32)
    return mul(lh, rh) + mul(ll, rh) + mul(lh, rl)


def kernel_body(
    n_sens, n_par, chunks,
    probes, kern, noise, weight, out,
    gath, field, fe_h, fe_l, fo_h, fo_l, stage, k_h, k_l,
    obs, rs_buf, full, we_h, we_l, wo_h, wo_l, mix_h, mix_l, acc, fin,
    k_sem, g_send, g_recv, rs_send, rs_recv, ag_send, ag_recv, f_send, f_recv,
):
    steps, par_rows, sensors = kern.shape
    columns = acc.shape[0]
    p_count = columns // steps
    width = sensors // chunks
    groups = steps // LAGS
    span = LAGS * p_count
    own_cols = probes.shape[1]
    piece = columns // n_par
    par, sens = lax.axis_index("par"), lax.axis_index("sens")

    def fetch(chunk, group, slot):
        return pltpu.make_async_copy(
            kern.at[pl.ds(group * LAGS, LAGS), :, pl.ds(pl.multiple_of(chunk * width, width), width)],
            stage.at[slot], k_sem.at[slot])

    for n in range(SLOTS):
        fetch(n // groups, n % groups, n % SLOTS).start()

    barrier = pltpu.get_barrier_semaphore()
    for k in range(1, n_par):
        pl.semaphore_signal(barrier, inc=1, device_id={"par": lax.rem(par + k, n_par)}, device_id_type=MESH)
    for k in range(1, n_sens):
        pl.semaphore_signal(barrier, inc=1, device_id={"sens": lax.rem(sens + k, n_sens)}, device_id_type=MESH)
    pl.semaphore_wait(barrier, n_par + n_sens - 2)

    gathers = [
        pltpu.make_async_remote_copy(
            src_ref=probes, dst_ref=gath.at[sens], send_sem=g_send.at[k], recv_sem=g_recv.at[k],
            device_id={"sens": lax.rem(sens + k, n_sens)}, device_id_type=MESH)
        for k in range(1, n_sens)
    ]
    for copy in gathers:
        copy.start()
    gath[sens] = probes[...]

    def split_lag(slot, i, lag, chunk):
        high, low = split(stage[slot, i])
        rows = pl.ds(pl.multiple_of(lag * par_rows, par_rows), par_rows)
        cols = pl.ds(chunk * width, width)
        k_h[rows, cols] = high
        k_l[rows, cols] = low

    row_t = lax.broadcasted_iota(jnp.int32, (columns, steps), 0) // p_count
    spread = (row_t == lax.broadcasted_iota(jnp.int32, (columns, steps), 1)).astype(BF16)
    same = (
        lax.broadcasted_iota(jnp.int32, (columns, columns), 0) % p_count
        == lax.broadcasted_iota(jnp.int32, (columns, columns), 1) % p_count
    )
    for part, mix in zip(split(noise[...]), (mix_h, mix_l)):
        rows = jnp.dot(spread, part, preferred_element_type=F32).astype(BF16)
        both = lax.dot_general(rows, spread, (((1,), (1,)), ((), ())), preferred_element_type=F32)
        mix[...] = jnp.where(same, both, 0.0).astype(BF16)

    zero_pad = jnp.zeros((span, par_rows), BF16)
    field[0:span, :] = jnp.zeros((span, par_rows), F32)
    for ref in (fe_h, fe_l, fo_h, fo_l):
        ref[0:span, :] = zero_pad
    for ref in (we_h, we_l, wo_h, wo_l):
        ref[columns:columns + span, :] = jnp.zeros((span, width), BF16)

    def first_splits(g, carry):
        slot = lax.rem(g, SLOTS)
        fetch(0, g, slot).wait()
        for i in range(LAGS):
            split_lag(slot, i, g * LAGS + i, 0)
        nxt = g + SLOTS
        fetch(nxt // groups, lax.rem(nxt, groups), slot).start()
        return carry

    lax.fori_loop(0, groups, first_splits, 0)

    for copy in gathers:
        copy.wait()
    for b in range(n_sens):
        field[span + b * own_cols:span + (b + 1) * own_cols, :] = gath[b].T
    fe_h[span:, :], fe_l[span:, :] = split(field[span:, :])
    fo_h[span:, :], fo_l[span:, :] = split(field[span - p_count:span - p_count + columns, :])

    def forward(chunk, g):
        start = span * g
        rows = columns - start
        left_h, left_l = [], []
        for i in range(LAGS):
            at = span - p_count * (i - i % 2)
            hi, lo = (fo_h, fo_l) if i % 2 else (fe_h, fe_l)
            left_h.append(hi[at:at + rows, :])
            left_l.append(lo[at:at + rows, :])
        lags = slice(g * LAGS * par_rows, (g + 1) * LAGS * par_rows)
        cols = slice(chunk * width, (chunk + 1) * width)
        term = dot3((jnp.concatenate(left_h, 1), jnp.concatenate(left_l, 1)), (k_h[lags, cols], k_l[lags, cols]))
        if g == 0:
            obs[chunk] = term
        else:
            obs[chunk, start:, :] += term

    def backward(chunk, g):
        start = span * g
        rows = columns - start
        left_h, left_l, right_h, right_l = [], [], [], []
        cols = slice(chunk * width, (chunk + 1) * width)
        for i in range(LAGS):
            at = start + p_count * (i - i % 2)
            hi, lo = (wo_h, wo_l) if i % 2 else (we_h, we_l)
            left_h.append(hi[at:at + rows, :])
            left_l.append(lo[at:at + rows, :])
            lag = slice((g * LAGS + i) * par_rows, (g * LAGS + i + 1) * par_rows)
            right_h.append(k_h[lag, cols])
            right_l.append(k_l[lag, cols])
        term = dot3(
            (jnp.concatenate(left_h, 1), jnp.concatenate(left_l, 1)),
            (jnp.concatenate(right_h, 1), jnp.concatenate(right_l, 1)), True)
        if g == 0 and chunk == 0:
            acc[...] = term
        else:
            acc[0:rows, :] += term

    def piece_of(index):
        return pl.ds(pl.multiple_of(index * piece, piece), piece)

    def scatter(chunk):
        copies = []
        for k in range(1, n_par):
            peer = lax.rem(par + k, n_par)
            copies.append(pltpu.make_async_remote_copy(
                src_ref=obs.at[chunk, piece_of(peer)], dst_ref=rs_buf.at[chunk, k],
                send_sem=rs_send.at[chunk, k], recv_sem=rs_recv.at[chunk, k],
                device_id={"par": peer}, device_id_type=MESH))
        for copy in copies:
            copy.start()
        return copies

    def reduce_and_spread(chunk, scatters):
        total = obs[chunk, piece_of(par)]
        for k, copy in enumerate(scatters, 1):
            copy.wait()
            total = total + rs_buf[chunk, k]
        full[chunk, piece_of(par)] = total
        copies = [
            pltpu.make_async_remote_copy(
                src_ref=full.at[chunk, piece_of(par)], dst_ref=full.at[chunk, piece_of(par)],
                send_sem=ag_send.at[chunk, k], recv_sem=ag_recv.at[chunk, k],
                device_id={"par": lax.rem(par + k, n_par)}, device_id_type=MESH)
            for k in range(1, n_par)
        ]
        for copy in copies:
            copy.start()
        return copies

    def weigh(chunk, spreads):
        for copy in spreads:
            copy.wait()
        mixed = dot3((mix_h[...], mix_l[...]), split(full[chunk]))
        mixed = mixed * weight[0:1, chunk * width:(chunk + 1) * width]
        we_h[0:columns, :], we_l[0:columns, :] = split(mixed)
        later = jnp.concatenate([mixed[p_count:], jnp.zeros((p_count, width), F32)], 0)
        wo_h[0:columns, :], wo_l[0:columns, :] = split(later)

    middle = 6 * groups // 16
    spreads = None
    scatters = None
    for chunk in range(chunks):
        for g in range(groups):
            if chunk > 0 and g == middle:
                spreads = reduce_and_spread(chunk - 1, scatters)
            if chunk + 1 < chunks:
                n = (chunk + 1) * groups + g
                fetch(chunk + 1, g, n % SLOTS).wait()
                for i in range(LAGS):
                    split_lag(n % SLOTS, i, g * LAGS + i, chunk + 1)
                nxt = n + SLOTS
                if nxt < chunks * groups:
                    fetch(nxt // groups, nxt % groups, nxt % SLOTS).start()
            forward(chunk, g)
        scatters = scatter(chunk)
    weigh(0, spreads)
    for g in range(groups):
        if g == middle:
            spreads = reduce_and_spread(1, scatters)
        backward(0, g)
    weigh(1, spreads)
    for g in range(groups):
        backward(1, g)

    def own_block(index):
        return pl.ds(pl.multiple_of(index * own_cols, own_cols), own_cols)

    finals = []
    for k in range(1, n_sens):
        peer = lax.rem(sens + k, n_sens)
        finals.append(pltpu.make_async_remote_copy(
            src_ref=acc.at[own_block(peer)], dst_ref=fin.at[k],
            send_sem=f_send.at[k], recv_sem=f_recv.at[k],
            device_id={"sens": peer}, device_id_type=MESH))
    for copy in finals:
        copy.start()
    total = acc[own_block(sens)]
    for k, copy in enumerate(finals, 1):
        copy.wait()
        total = total + fin[k]
    out[...] = total.T


def per_device(n_sens, n_par, probes, kern, noise, weight):
    steps, par_rows, sensors = kern.shape
    own_cols = probes.shape[1]
    columns = own_cols * n_sens
    p_count = columns // steps
    chunks = 2
    width = sensors // chunks
    span = LAGS * p_count
    piece = columns // n_par
    vmem, dma = pltpu.VMEM, pltpu.SemaphoreType.DMA
    in_vmem = pl.BlockSpec(memory_space=pltpu.VMEM)
    field = vmem((span + columns, par_rows), BF16)
    weighted = vmem((columns + span, width), BF16)
    whole = vmem((steps * par_rows, sensors), BF16)
    mix = vmem((columns, columns), BF16)
    return pl.pallas_call(
        functools.partial(kernel_body, n_sens, n_par, chunks),
        out_shape=jax.ShapeDtypeStruct(probes.shape, F32),
        in_specs=[in_vmem, pl.BlockSpec(memory_space=pl.ANY), in_vmem, in_vmem],
        out_specs=in_vmem,
        scratch_shapes=[
            vmem((n_sens, par_rows, own_cols), F32), vmem((span + columns, par_rows), F32),
            field, field, field, field,
            vmem((SLOTS, LAGS, par_rows, width), F32), whole, whole,
            vmem((chunks, columns, width), F32), vmem((chunks, n_par, piece, width), F32),
            vmem((chunks, columns, width), F32),
            weighted, weighted, weighted, weighted, mix, mix,
            vmem((columns, par_rows), F32), vmem((n_sens, own_cols, par_rows), F32),
            dma((SLOTS,)), dma((n_sens,)), dma((n_sens,)),
            dma((chunks, n_par)), dma((chunks, n_par)), dma((chunks, n_par)), dma((chunks, n_par)),
            dma((n_sens,)), dma((n_sens,)),
        ],
        compiler_params=pltpu.CompilerParams(
            collective_id=0, has_side_effects=True, vmem_limit_bytes=60 * 1024 * 1024),
    )(probes, kern, noise, weight.reshape(1, sensors))


def solution(mesh):
    placed = (P("par", "sens"), P(None, "par", "sens"), P(), P("sens"))
    body = functools.partial(per_device, mesh.shape["sens"], mesh.shape["par"])
    return jax.shard_map(body, mesh=mesh, in_specs=placed, out_specs=P("par", "sens"), check_vma=False)
```

time: 386 us -> 101 us (0.26)
  local copies, waits for them, and re-layouts: 126 us -> 1.57 us
  matrix products: 124 us -> 0 us
  Pallas kernels: 0 us -> 99.3 us
  waiting for transfers between devices: 99.1 us -> 0 us
  between operations: 13.5 us -> 0.01 us
  other arithmetic: 12.7 us -> 0 us
  blocking collectives: 7.49 us -> 0 us
    dot_general x3 -> x0, matrix products: 124 us -> none  [the longest x1 63.4 us: per_device(): jnp.dot(kernel_flat, weighted, precision=highest, preferred_element_type=...]
    pallas_call x0 -> x1, Pallas kernels: none -> 99.3 us  [per_device(): pl.pallas_call(functools.partial(kernel_body, n_sens, n_par, chunks), out...]
    psum x1 -> x0, waiting for transfers between devices: 76.8 us -> none  [per_device(): lax.psum(lax.dot_general(kernel_flat, shifted, (((0,), (0,)), ((), ())),...]
    gather x3 -> x0, local copies, waits for them, and re-layouts: 64.3 us -> none  [the longest x2 40.6 us: per_device(): lax.dynamic_slice_in_dim(padded, time_steps - lag_index, time_steps, 1)]
    pad x2 -> x0, local copies, waits for them, and re-layouts: 32.7 us -> none  [the longest x1 32.6 us: per_device(): spread = jnp.pad(spread, ((0, 0), (0, 0), (0, time_steps), (0, 0)))]
    unnamed x7 -> x1, local copies, waits for them, and re-layouts: 25.6 us -> 1.57 us
    reduce_scatter x1 -> x0, waiting for transfers between devices: 22.3 us -> none  [per_device(): lax.psum_scatter(partial_action, 'sens', scatter_dimension=1, tiled=True)]
    reduce_sum x1 -> x0, other arithmetic: 12.7 us -> none  [per_device(): partial_action = jnp.sum(earlier, axis=0).reshape(par_rows, columns)]
  transfers between devices with their start and end apart: 2 -> 0, of which waited for: 2 -> 0; matrix products, arithmetic and copies ran while one was open for 0% -> 0% of each run, Pallas kernels for 0% -> 0%
where the time goes in v1:
time: 101 us
  Pallas kernels  99.3 us (98%)
  local copies, waits for them, and re-layouts  1.57 us (2%)
    pallas_call x1, Pallas kernels, per_device(): pl.pallas_call(functools.partial(kernel_body, n_sens, n_par, chunks), out...  99.3 us

profile of v1, /device:TPU:31, one launch (start us, length us, event | category | flops | bytes accessed | tf_op | source)
XLA Modules:
  0.0 100.8 jit_solution(5041603562517789899)
XLA Ops:
  0.0 99.3 %shard_map.46 = f32[256,128]{1,0:T(8,128)} custom-call(f32[256,128]{1,0:T(8,128)} %probes.1, f32[64,256,512]{2,1,0:T(8,128)} %kern.1, f32[64,64]{1,0:T(8,128)} %noise.1, f32[1,512]{1,0:T(1,128)} %bitcast.1), custom_call_target="tpu_custom_call" | custom-call | tf_op jit(solution)/shard_map/pallas_call | solution.py:253
  99.3 1.6 %copy.6 = f32[256,128]{1,0:T(8,128)} copy(f32[256,128]{1,0:T(8,128)} %shard_map.46) | data formatting | bytes 262144

commit v2 on v1

--- a/solution.py
+++ b/solution.py
@@ -20,10 +20,11 @@
 
 
 def dot3(left, right, transposed=False):
-    dims = (((1,), (1 if transposed else 0,)), ((), ()))
+    side = 1 if transposed else 0
     (lh, ll), (rh, rl) = left, right
-    mul = functools.partial(lax.dot_general, dimension_numbers=dims, preferred_element_type=F32)
-    return mul(lh, rh) + mul(ll, rh) + mul(lh, rl)
+    return lax.dot_general(
+        jnp.concatenate(lh + ll + lh, 1), jnp.concatenate(rh + rh + rl, side),
+        dimension_numbers=(((1,), (side,)), ((), ())), preferred_element_type=F32)
 
 
 def kernel_body(
@@ -40,7 +41,7 @@
     groups = steps // LAGS
     span = LAGS * p_count
     own_cols = probes.shape[1]
-    piece = columns // n_par
+    piece = columns // (2 * n_par)
     par, sens = lax.axis_index("par"), lax.axis_index("sens")
 
     def fetch(chunk, group, slot):
@@ -58,14 +59,20 @@
         pl.semaphore_signal(barrier, inc=1, device_id={"sens": lax.rem(sens + k, n_sens)}, device_id_type=MESH)
     pl.semaphore_wait(barrier, n_par + n_sens - 2)
 
-    gathers = [
-        pltpu.make_async_remote_copy(
-            src_ref=probes, dst_ref=gath.at[sens], send_sem=g_send.at[k], recv_sem=g_recv.at[k],
-            device_id={"sens": lax.rem(sens + k, n_sens)}, device_id_type=MESH)
-        for k in range(1, n_sens)
-    ]
-    for copy in gathers:
-        copy.start()
+    twin = sens + 1 - 2 * lax.rem(sens, 2)
+    across = lax.rem(sens + 2, n_sens)
+    twin_across = lax.rem(twin + 2, n_sens)
+
+    def to_sens(src, dst, k, device):
+        return pltpu.make_async_remote_copy(
+            src_ref=src, dst_ref=dst, send_sem=g_send.at[k], recv_sem=g_recv.at[k],
+            device_id={"sens": device}, device_id_type=MESH)
+
+    own_across = to_sens(probes, gath.at[sens], 1, across)
+    own_twin = to_sens(probes, gath.at[sens], 0, twin)
+    handed = to_sens(gath.at[across], gath.at[across], 2, twin)
+    own_across.start()
+    own_twin.start()
     gath[sens] = probes[...]
 
     def split_lag(slot, i, lag, chunk):
@@ -102,10 +109,13 @@
         fetch(nxt // groups, lax.rem(nxt, groups), slot).start()
         return carry
 
-    lax.fori_loop(0, groups, first_splits, 0)
-
-    for copy in gathers:
-        copy.wait()
+    lax.fori_loop(0, 5 * groups // 8, first_splits, 0)
+    own_across.wait_recv()
+    handed.start()
+    lax.fori_loop(5 * groups // 8, groups, first_splits, 0)
+    own_across.wait_send()
+    own_twin.wait()
+    handed.wait()
     for b in range(n_sens):
         field[span + b * own_cols:span + (b + 1) * own_cols, :] = gath[b].T
     fe_h[span:, :], fe_l[span:, :] = split(field[span:, :])
@@ -120,9 +130,13 @@
             hi, lo = (fo_h, fo_l) if i % 2 else (fe_h, fe_l)
             left_h.append(hi[at:at + rows, :])
             left_l.append(lo[at:at + rows, :])
-        lags = slice(g * LAGS * par_rows, (g + 1) * LAGS * par_rows)
         cols = slice(chunk * width, (chunk + 1) * width)
-        term = dot3((jnp.concatenate(left_h, 1), jnp.concatenate(left_l, 1)), (k_h[lags, cols], k_l[lags, cols]))
+        term = None
+        for at in range(0, LAGS, LAGS // 2):
+            part = slice(at, at + LAGS // 2)
+            lags = slice((g * LAGS + part.start) * par_rows, (g * LAGS + part.stop) * par_rows)
+            product = dot3((left_h[part], left_l[part]), ([k_h[lags, cols]], [k_l[lags, cols]]))
+            term = product if term is None else term + product
         if g == 0:
             obs[chunk] = term
         else:
@@ -141,39 +155,41 @@
             lag = slice((g * LAGS + i) * par_rows, (g * LAGS + i + 1) * par_rows)
             right_h.append(k_h[lag, cols])
             right_l.append(k_l[lag, cols])
-        term = dot3(
-            (jnp.concatenate(left_h, 1), jnp.concatenate(left_l, 1)),
-            (jnp.concatenate(right_h, 1), jnp.concatenate(right_l, 1)), True)
+        term = None
+        for at in range(0, LAGS, LAGS // 2):
+            part = slice(at, at + LAGS // 2)
+            product = dot3((left_h[part], left_l[part]), (right_h[part], right_l[part]), True)
+            term = product if term is None else term + product
         if g == 0 and chunk == 0:
             acc[...] = term
         else:
             acc[0:rows, :] += term
 
-    def piece_of(index):
-        return pl.ds(pl.multiple_of(index * piece, piece), piece)
-
-    def scatter(chunk):
+    def piece_of(half, index):
+        return pl.ds(pl.multiple_of(half * (columns // 2) + index * piece, piece), piece)
+
+    def scatter(chunk, half):
         copies = []
         for k in range(1, n_par):
             peer = lax.rem(par + k, n_par)
             copies.append(pltpu.make_async_remote_copy(
-                src_ref=obs.at[chunk, piece_of(peer)], dst_ref=rs_buf.at[chunk, k],
-                send_sem=rs_send.at[chunk, k], recv_sem=rs_recv.at[chunk, k],
+                src_ref=obs.at[chunk, piece_of(half, peer)], dst_ref=rs_buf.at[chunk, half, k],
+                send_sem=rs_send.at[chunk, half, k], recv_sem=rs_recv.at[chunk, half, k],
                 device_id={"par": peer}, device_id_type=MESH))
         for copy in copies:
             copy.start()
         return copies
 
-    def reduce_and_spread(chunk, scatters):
-        total = obs[chunk, piece_of(par)]
+    def reduce_and_spread(chunk, half, scatters):
+        total = obs[chunk, piece_of(half, par)]
         for k, copy in enumerate(scatters, 1):
             copy.wait()
-            total = total + rs_buf[chunk, k]
-        full[chunk, piece_of(par)] = total
+            total = total + rs_buf[chunk, half, k]
+        full[chunk, piece_of(half, par)] = total
         copies = [
             pltpu.make_async_remote_copy(
-                src_ref=full.at[chunk, piece_of(par)], dst_ref=full.at[chunk, piece_of(par)],
-                send_sem=ag_send.at[chunk, k], recv_sem=ag_recv.at[chunk, k],
+                src_ref=full.at[chunk, piece_of(half, par)], dst_ref=full.at[chunk, piece_of(half, par)],
+                send_sem=ag_send.at[chunk, half, k], recv_sem=ag_recv.at[chunk, half, k],
                 device_id={"par": lax.rem(par + k, n_par)}, device_id_type=MESH)
             for k in range(1, n_par)
         ]
@@ -184,19 +200,23 @@
     def weigh(chunk, spreads):
         for copy in spreads:
             copy.wait()
-        mixed = dot3((mix_h[...], mix_l[...]), split(full[chunk]))
+        high, low = split(full[chunk])
+        mixed = dot3(([mix_h[...]], [mix_l[...]]), ([high], [low]))
         mixed = mixed * weight[0:1, chunk * width:(chunk + 1) * width]
         we_h[0:columns, :], we_l[0:columns, :] = split(mixed)
         later = jnp.concatenate([mixed[p_count:], jnp.zeros((p_count, width), F32)], 0)
         wo_h[0:columns, :], wo_l[0:columns, :] = split(later)
 
-    middle = 6 * groups // 16
-    spreads = None
-    scatters = None
+    first_half = groups // 2
+    turns = (groups // 8, 7 * groups // 16)
+    sent = {}
     for chunk in range(chunks):
         for g in range(groups):
-            if chunk > 0 and g == middle:
-                spreads = reduce_and_spread(chunk - 1, scatters)
+            for half, turn in enumerate(turns):
+                if chunk > 0 and g == turn:
+                    sent[half] = reduce_and_spread(chunk - 1, half, sent[half])
+            if g == first_half:
+                early = scatter(chunk, 0)
             if chunk + 1 < chunks:
                 n = (chunk + 1) * groups + g
                 fetch(chunk + 1, g, n % SLOTS).wait()
@@ -206,33 +226,39 @@
                 if nxt < chunks * groups:
                     fetch(nxt // groups, nxt % groups, nxt % SLOTS).start()
             forward(chunk, g)
-        scatters = scatter(chunk)
+        if chunk > 0:
+            spreads = sent[0] + sent[1]
+        sent = {0: early, 1: scatter(chunk, 1)}
     weigh(0, spreads)
     for g in range(groups):
-        if g == middle:
-            spreads = reduce_and_spread(1, scatters)
+        for half, turn in enumerate(turns):
+            if g == turn:
+                sent[half] = reduce_and_spread(1, half, sent[half])
         backward(0, g)
-    weigh(1, spreads)
+    weigh(1, sent[0] + sent[1])
     for g in range(groups):
         backward(1, g)
 
     def own_block(index):
         return pl.ds(pl.multiple_of(index * own_cols, own_cols), own_cols)
 
-    finals = []
-    for k in range(1, n_sens):
-        peer = lax.rem(sens + k, n_sens)
-        finals.append(pltpu.make_async_remote_copy(
-            src_ref=acc.at[own_block(peer)], dst_ref=fin.at[k],
-            send_sem=f_send.at[k], recv_sem=f_recv.at[k],
-            device_id={"sens": peer}, device_id_type=MESH))
-    for copy in finals:
-        copy.start()
-    total = acc[own_block(sens)]
-    for k, copy in enumerate(finals, 1):
-        copy.wait()
-        total = total + fin[k]
-    out[...] = total.T
+    def final(src, dst, k, device):
+        return pltpu.make_async_remote_copy(
+            src_ref=src, dst_ref=dst, send_sem=f_send.at[k], recv_sem=f_recv.at[k],
+            device_id={"sens": device}, device_id_type=MESH)
+
+    far = final(acc.at[own_block(twin_across)], fin.at[0], 0, twin)
+    near = final(acc.at[own_block(twin)], fin.at[1], 1, twin)
+    far.start()
+    near.start()
+    far.wait()
+    fin[2] = acc[own_block(across)] + fin[0]
+    last = final(fin.at[2], fin.at[3], 2, across)
+    last.start()
+    near.wait()
+    total = acc[own_block(sens)] + fin[1]
+    last.wait()
+    out[...] = (total + fin[3]).T
 
 
 def per_device(n_sens, n_par, probes, kern, noise, weight):
@@ -243,7 +269,7 @@
     chunks = 2
     width = sensors // chunks
     span = LAGS * p_count
-    piece = columns // n_par
+    piece = columns // (2 * n_par)
     vmem, dma = pltpu.VMEM, pltpu.SemaphoreType.DMA
     in_vmem = pl.BlockSpec(memory_space=pltpu.VMEM)
     field = vmem((span + columns, par_rows), BF16)
@@ -259,12 +285,12 @@
             vmem((n_sens, par_rows, own_cols), F32), vmem((span + columns, par_rows), F32),
             field, field, field, field,
             vmem((SLOTS, LAGS, par_rows, width), F32), whole, whole,
-            vmem((chunks, columns, width), F32), vmem((chunks, n_par, piece, width), F32),
+            vmem((chunks, columns, width), F32), vmem((chunks, 2, n_par, piece, width), F32),
             vmem((chunks, columns, width), F32),
             weighted, weighted, weighted, weighted, mix, mix,
-            vmem((columns, par_rows), F32), vmem((n_sens, own_cols, par_rows), F32),
+            vmem((columns, par_rows), F32), vmem((4, own_cols, par_rows), F32),
             dma((SLOTS,)), dma((n_sens,)), dma((n_sens,)),
-            dma((chunks, n_par)), dma((chunks, n_par)), dma((chunks, n_par)), dma((chunks, n_par)),
+            dma((chunks, 2, n_par)), dma((chunks, 2, n_par)), dma((chunks, 2, n_par)), dma((chunks, 2, n_par)),
             dma((n_sens,)), dma((n_sens,)),
         ],
         compiler_params=pltpu.CompilerParams(

time: 101 us -> 93.1 us (0.922)
  Pallas kernels: 99.3 us -> 90.4 us
    pallas_call x1, Pallas kernels: 99.3 us -> 90.4 us  [per_device(): pl.pallas_call(functools.partial(kernel_body, n_sens, n_par, chunks), out...]
where the time goes in v2:
time: 93.1 us; the launch traced here: 92 us
  Pallas kernels  90.4 us (97%)
  local copies, waits for them, and re-layouts  1.57 us (2%)
    pallas_call x1, Pallas kernels, per_device(): pl.pallas_call(functools.partial(kernel_body, n_sens, n_par, chunks), out...  90.4 us

profile of v2, /device:TPU:31, one launch (start us, length us, event | category | flops | bytes accessed | tf_op | source)
XLA Modules:
  0.0 92.0 jit_solution(11943842276005308110)
XLA Ops:
  0.0 90.4 %shard_map.46 = f32[256,128]{1,0:T(8,128)} custom-call(f32[256,128]{1,0:T(8,128)} %probes.1, f32[64,256,512]{2,1,0:T(8,128)} %kern.1, f32[64,64]{1,0:T(8,128)} %noise.1, f32[1,512]{1,0:T(1,128)} %bitcast.1), custom_call_target="tpu_custom_call" | custom-call | tf_op jit(solution)/shard_map/pallas_call | solution.py:279
  90.4 1.6 %copy.6 = f32[256,128]{1,0:T(8,128)} copy(f32[256,128]{1,0:T(8,128)} %shard_map.46) | data formatting | bytes 262144
